TPU v7x, 128 devices: a whole 4x4x4 slice. The times are simulated.
128 devices in a mesh: grp: 8 (over z, core), ep: 16 (over x, y).
Axes of the slice: x: 4, y: 4, z: 4, core: 2. Of those that a mesh axis runs over, the one named last changes fastest.
Arguments:
- hidden_in: bfloat16 [16384, 2048], P(('grp', 'ep')), may hold values from -24 to 24
- prompt_lengths: int32 [8, 5], P('grp'), may hold values from 1 to 1024, 2048 in all within a row
- routes: int32 [16384, 6], P(('grp', 'ep')), may hold values from 0 to 63, all different within a row; in each aligned block of 128 rows (0 to 127, 128 to 255, ...) at most 16 rows name the same one
- route_weights: float32 [16384, 6], P(('grp', 'ep')), may hold values from 0.05 to 0.4
- w_query: bfloat16 [2048, 2048], P(None, 'ep'), may hold values from -3 to 3
- w_key: bfloat16 [2048, 2048], P(None, 'ep'), may hold values from -3 to 3
- w_value: bfloat16 [2048, 2048], P(None, 'ep'), may hold values from -0.125 to 0.125
- w_out: bfloat16 [2048, 2048], replicated, may hold values from -0.125 to 0.125
- shared_gate: bfloat16 [2048, 2816], P(None, 'grp'), may hold values from -0.125 to 0.125
- shared_up: bfloat16 [2048, 2816], P(None, 'grp'), may hold values from -0.125 to 0.125
- shared_down: bfloat16 [2816, 2048], P('grp'), may hold values from -0.109375 to 0.109375
- expert_gate: bfloat16 [128, 2048, 704], P(('grp', 'ep')), may hold values from -0.125 to 0.125
- expert_up: bfloat16 [128, 2048, 704], P(('grp', 'ep')), may hold values from -0.125 to 0.125
- expert_down: bfloat16 [128, 704, 2048], P(('grp', 'ep')), may hold values from -0.15625 to 0.15625
Outputs:
- attended: bfloat16 [16384, 2048], P(('grp', 'ep'))
- moe_update: bfloat16 [16384, 2048], P(('grp', 'ep'))
Inputs may be any that keep to these rules, and one draw needn't show every extreme that they name: `routes`: each row names 6 different experts. The 128 rows of one device name any one expert at most 16 times, and in every draw some device names some expert exactly 16 times. `prompt_lengths`: row g describes group g: its first 4 entries are the lengths of the packed prompts in order, the last one the padding positions at the group's end. Each row sums to 2048, and its largest entry is 1024.
All inputs are finite; a program needn't handle non-finite values.
Results may differ from a plain program's by a relative error of at most 0.015.
The roundings to bfloat16 on the way count: a program that leaves them out, or rounds other values in their place, can miss the bound.
Values may be sent and summed in bfloat16 or wider, within the bound.
A program may use at most 128 MiB of HBM per device.

v0:
```python
import math
import jax
import jax.numpy as jnp
from jax import lax
from jax.sharding import PartitionSpec as P

HDIM = 128
epsilon = 1e-06


def rms_rows(values):
    mean_square = jnp.mean(values * values, axis=-1, keepdims=True)
    return values * lax.rsqrt(mean_square + epsilon)


def segment_ids(length_row, row_total):
    prompt_ends = jnp.cumsum(length_row[:-1])
    positions = jnp.arange(row_total, dtype=jnp.int32)
    segment = jnp.sum((positions[:, None] >= prompt_ends[None, :]).astype(jnp.int32), axis=1)
    return jnp.where(segment >= length_row.shape[0] - 1, -1, segment)


def attend(queries, key_rows, value_rows, segment, block_rows):
    row_total, heads_here, head_dim = queries.shape
    score_scale = 1.0 / math.sqrt(head_dim)
    positions = jnp.arange(row_total, dtype=jnp.int32)

    def one_block(first_row):
        query_block = lax.dynamic_slice_in_dim(queries, first_row, block_rows, 0)
        query_pos = first_row + jnp.arange(block_rows, dtype=jnp.int32)
        query_seg = lax.dynamic_slice_in_dim(segment, first_row, block_rows, 0)
        scores = (
            jnp.einsum("qhd,khd->hqk", query_block, key_rows, preferred_element_type=jnp.float32)
            * score_scale
        )
        allowed = (
            (positions[None, :] <= query_pos[:, None])
            & (segment[None, :] == query_seg[:, None])
            & ((query_seg[:, None] >= 0) | (positions[None, :] == query_pos[:, None]))
        )
        scores = jnp.where(allowed[None], scores, -1e30)
        largest = jnp.max(scores, axis=2, keepdims=True)
        weights = jnp.where(allowed[None], jnp.exp(scores - largest), 0.0)
        totals = jnp.sum(weights, axis=2, keepdims=True)
        attn_probs = (weights / totals).astype(jnp.bfloat16)
        mixed_rows = jnp.einsum(
            "hqk,khd->qhd", attn_probs, value_rows, preferred_element_type=jnp.float32
        )
        return mixed_rows.astype(jnp.bfloat16)

    starts = jnp.arange(row_total // block_rows, dtype=jnp.int32) * block_rows
    blocks = lax.map(one_block, starts)
    return blocks.reshape(row_total, heads_here * head_dim)


def expert_rows(received, gate_half, up_half, down_half):
    width = received.shape[2]
    flattened = received.reshape(-1, width)
    gate_act = jnp.dot(flattened, gate_half, preferred_element_type=jnp.float32)
    up_act = jnp.dot(flattened, up_half, preferred_element_type=jnp.float32)
    hidden = (jax.nn.silu(gate_act) * up_act).astype(jnp.bfloat16)
    partial_value = jnp.dot(hidden, down_half, preferred_element_type=jnp.float32).astype(
        jnp.bfloat16
    )
    return partial_value.reshape(received.shape)


def local(
    hidden_in,
    prompt_lengths,
    routes,
    route_weights,
    w_query,
    w_key,
    w_value,
    w_out,
    shared_gate,
    shared_up,
    shared_down,
    expert_gate,
    expert_up,
    expert_down,
):
    tok_rows, width = hidden_in.shape
    top_count = routes.shape[1]
    grp_count = lax.axis_size("grp")
    ep_count = lax.axis_size("ep")
    device_count = grp_count * ep_count
    expert_count = device_count // 2
    capacity = 8 * tok_rows // expert_count
    group_rows = tok_rows * ep_count
    local_width = w_query.shape[1]
    heads_here = local_width // HDIM
    normed = rms_rows(hidden_in.astype(jnp.float32)).astype(jnp.bfloat16)
    w_joined = jnp.concatenate((w_query, w_key, w_value), axis=1)
    joined = jnp.dot(
        lax.all_gather(normed, "ep", axis=0, tiled=True),
        w_joined,
        preferred_element_type=jnp.float32,
    ).astype(jnp.bfloat16)
    queries = joined[:, :local_width].reshape(group_rows, heads_here, HDIM)
    key_rows = joined[:, local_width : 2 * local_width].reshape(group_rows, heads_here, HDIM)
    value_rows = joined[:, 2 * local_width :].reshape(group_rows, heads_here, HDIM)
    segment = segment_ids(prompt_lengths[0], group_rows)
    heads_local = attend(queries, key_rows, value_rows, segment, min(512, group_rows))
    heads_out = lax.all_to_all(heads_local, "ep", split_axis=0, concat_axis=1, tiled=True)
    residual = hidden_in.astype(jnp.float32) + jnp.dot(
        heads_out, w_out, preferred_element_type=jnp.float32
    )
    normed_moe = rms_rows(residual).astype(jnp.bfloat16)
    gathered = lax.all_gather(normed_moe, "grp", axis=0, tiled=True)
    gate_act = jnp.dot(gathered, shared_gate, preferred_element_type=jnp.float32)
    up_act = jnp.dot(gathered, shared_up, preferred_element_type=jnp.float32)
    hidden = (jax.nn.silu(gate_act) * up_act).astype(jnp.bfloat16)
    shared_out = lax.psum_scatter(
        jnp.dot(hidden, shared_down, preferred_element_type=jnp.float32).astype(jnp.bfloat16),
        "grp",
        scatter_dimension=0,
        tiled=True,
    ).astype(jnp.float32)
    flat_experts = routes.reshape(-1)
    route_total = flat_experts.shape[0]
    onehot = (flat_experts[:, None] == jnp.arange(expert_count, dtype=jnp.int32)[None, :]).astype(
        jnp.int32
    )
    rank_in = jnp.sum((jnp.cumsum(onehot, axis=0) - onehot) * onehot, axis=1)
    slot_index = flat_experts * capacity + rank_in
    token_index = jnp.arange(route_total, dtype=jnp.int32) // top_count
    slot_source = (
        jnp.full((expert_count * capacity,), tok_rows, jnp.int32).at[slot_index].set(token_index)
    )
    padded_rows = jnp.concatenate((normed_moe, jnp.zeros((1, width), jnp.bfloat16)), axis=0)
    outbound = padded_rows[slot_source].reshape(expert_count, 1, capacity, width)
    outbound = jnp.broadcast_to(outbound, (expert_count, 2, capacity, width)).reshape(
        device_count, capacity, width
    )
    gate_half = expert_gate[0]
    up_half = expert_up[0]
    down_half = expert_down[0]
    returned = lax.all_to_all(
        expert_rows(
            lax.all_to_all(outbound, ("grp", "ep"), split_axis=0, concat_axis=0, tiled=True),
            gate_half,
            up_half,
            down_half,
        ),
        ("grp", "ep"),
        split_axis=0,
        concat_axis=0,
        tiled=True,
    )
    by_expert = returned.reshape(expert_count, 2, capacity, width)
    first_half = by_expert[flat_experts, 0, rank_in]
    second_half = by_expert[flat_experts, 1, rank_in]
    expert_sum = first_half.astype(jnp.float32) + second_half.astype(jnp.float32)
    weighted = expert_sum * route_weights.reshape(-1, 1)
    routed = jnp.sum(weighted.reshape(tok_rows, top_count, width), axis=1)
    attended = residual.astype(jnp.bfloat16)
    moe_update = (shared_out + routed).astype(jnp.bfloat16)
    return (attended, moe_update)


def solution(mesh):
    in_specs = (
        P(("grp", "ep"), None),
        P("grp", None),
        P(("grp", "ep"), None),
        P(("grp", "ep"), None),
        P(None, "ep"),
        P(None, "ep"),
        P(None, "ep"),
        P(),
        P(None, "grp"),
        P(None, "grp"),
        P("grp", None),
        P(("grp", "ep"), None, None),
        P(("grp", "ep"), None, None),
        P(("grp", "ep"), None, None),
    )
    out_specs = (P(("grp", "ep"), None), P(("grp", "ep"), None))
    return jax.shard_map(local, mesh=mesh, in_specs=in_specs, out_specs=out_specs, check_vma=False)
```

profile of v0, /device:TPU:37, one launch (start us, length us, event | category | flops | bytes accessed | tf_op | source)
XLA Modules:
  0.0 498.3 jit_solution(996202673333153389)
XLA Ops:
  7.2 1.4 fusion.33
  8.6 2.0 fusion.34
  10.6 0.7 slice_bitcast_fusion.3
  11.3 0.2 reduce-window.18
  11.5 0.8 copy.32
  12.3 0.1 eq.51
  12.4 1.8 reduce-window.19
  14.3 0.1 convert_reduce_fusion
  14.3 0.3 slice_reduce_fusion
  14.6 68.6 %all-gather.3.cloned.1.call-done = bf16[2048,2048]{1,0:T(8,128)(2,1)} async-done(((bf16[128,2048]{1,0:T(8,128)(2,1)}), bf16[2048,2048]{1,0:T(8,128)(2,1)}) %all-gather.3.cloned.1.call-update) | async-done | bytes 8388624 | tf_op jit(solution)/shard_map/all_gather | solution.py:97
  83.3 8.3 %convolution_convert_fusion.2 = bf16[2048,384]{1,0:T(8,128)(2,1)S(1)} fusion(bf16[2048,2048]{1,0:T(8,128)(2,1)} %all-gather.3.cloned.1.call-done, bf16[2048,128]{1,0:T(8,128)(2,1)} %param.22, bf16[2048,128]{1,0:T(8,128)(2,1)} %param.21, bf16[2048,128]{1,0:T(8,128)(2,1)} %param.20), kind=kOutput, calls=%fused_computation.40 | convolution fusion | flops 3226730496 | bytes 11534336 | tf_op jit(solution)/shard_map/dot_general | solution.py:96
  91.5 1.3 slice_bitcast_fusion
  92.8 53.6 %while.12 = (s32[]{:T(128)}, bf16[4,512,1,128]{3,1,2,0:T(8,128)(2,1)}, s32[4]{0:T(128)S(1)}, s32[2048]{0:T(1024)S(1)}, bf16[2048,1,128]{2,0,1:T(8,128)(2,1)}, /*...) while((s32[]{:T(128)}, ...), condition=%wide.region_6.7_spmd.clone.clone, body=%wide.region_3.6_spmd.clone.clone.sunk | while | flops 570490880 | bytes 16046279 | solution.py:52
  92.8 0.7 dynamic_slice.28
  95.5 0.1 broadcast_compare_fusion.2
  95.6 0.7 iota_add_fusion.2
  96.3 3.3 fusion.70
  99.6 2.9 fusion.71
  102.5 3.7 fusion.72
  106.2 0.7 dynamic_slice.28
  109.0 0.7 iota_add_fusion.2
  109.7 3.3 fusion.70
  113.0 2.9 fusion.71
  115.9 3.7 fusion.72
  119.6 0.7 dynamic_slice.28
  122.4 0.7 iota_add_fusion.2
  123.1 3.3 fusion.70
  126.4 2.9 fusion.71
  129.3 3.7 fusion.72
  133.0 0.7 dynamic_slice.28
  135.8 0.7 iota_add_fusion.2
  136.5 3.3 fusion.70
  139.8 2.9 fusion.71
  142.7 3.7 fusion.72
  146.4 5.5 %all-to-all-start = ((bf16[16,128,128]{2,1,0:T(8,128)(2,1)}), bf16[16,128,128]{2,1,0:T(8,128)(2,1)}, u32[]{:S(2)}, u32[]{:S(2)}) async-start(bf16[16,128,128]{2,1,0:T(8,128)(2,1)} %bitcast.95), calls=%async_computation | async-start | bytes 1048576 | tf_op jit(solution)/shard_map/all_to_all | solution.py:106
  151.9 0.1 eq.47
  152.1 0.1 reshape.218
  152.2 1.1 fusion.38
  153.3 3.4 scatter_custom_fusion
  156.7 3.3 all-to-all-done
  160.0 2.0 copy.31
  162.0 4.9 multiply_reduce_fusion.1
  167.0 1.1 multiply_convert_fusion.1
  168.1 1.1 concatenate.13
  169.2 6.0 %gather_fusion = bf16[1024,2048]{1,0:T(8,128)(2,1)} fusion(bf16[129,2048]{1,0:T(8,128)(2,1)S(1)} %concatenate.13, s32[1024]{0:T(1024)S(1)} %fusion.42), kind=kCustom, calls=%fused_computation | custom fusion | bytes 8392704 | tf_op jit(solution)/shard_map/gather | solution.py:133
  175.2 6.7 %broadcast_in_dim.43 = bf16[64,2,16,2048]{3,2,1,0:T(8,128)(2,1)} broadcast(bf16[64,16,2048]{2,1,0:T(8,128)(2,1)} %bitcast.92), dimensions={0,2,3} | broadcast | bytes 12582912 | tf_op jit(solution)/shard_map/broadcast_in_dim | solution.py:134
  181.9 10.4 %all-to-all-start.1 = ((bf16[128,16,2048]{2,1,0:T(8,128)(2,1)}), bf16[128,16,2048]{2,1,0:T(8,128)(2,1)}, u32[]{:S(2)}, u32[]{:S(2)}) async-start(bf16[128,16,2048]{2,1,0:T(8,128)(2,1)} %bitcast.91), calls=%async_computation.2 | async-start | bytes 16777216 | tf_op jit(solution)/shard_map/all_to_all | solution.py:142
  192.4 0.7 all-gather.5.cloned.1.call-update
  193.1 102.8 %all-to-all-done.1 = bf16[128,16,2048]{2,1,0:T(8,128)(2,1)} async-done(((bf16[128,16,2048]{2,1,0:T(8,128)(2,1)}), bf16[128,16,2048]{2,1,0:T(8,128)(2,1)}, u32[]{:S(2)}, u32[]{:S(2)}) %all-to-all-start.1) | async-done | bytes 8388640 | tf_op jit(solution)/shard_map/all_to_all | solution.py:142
  295.9 11.1 %fusion.24 = f32[2048,704]{0,1:T(8,128)} fusion(bf16[2048,2048]{1,0:T(8,128)(2,1)} %bitcast.11, bf16[1,2048,704]{1,2,0:T(8,128)(2,1)} %param.27), kind=kOutput, calls=%fused_computation.37 | convolution fusion | flops 5905580032 | bytes 17039360 | tf_op jit(solution)/shard_map/dot_general | solution.py:59
  307.0 19.1 %convolution_convert_fusion = bf16[2048,2048]{1,0:T(8,128)(2,1)} fusion(f32[2048,704]{0,1:T(8,128)} %fusion.24, bf16[2048,2048]{1,0:T(8,128)(2,1)} %bitcast.11, bf16[1,704,2048]{2,1,0:T(8,128)(2,1)S(1)} %copy-done, bf16[1,2048,704]{1,2,0:T(8,128)(2,1)} %param.28), kind=kOutput, calls=%fused_computation.31 | convolution fusion | flops 11824005120 | bytes 28311552 | tf_op jit(solution)/shard_map/dot_general | solution.py:62
  326.0 6.2 %all-to-all-start.2 = ((bf16[128,16,2048]{2,1,0:T(8,128)(2,1)}), bf16[128,16,2048]{2,1,0:T(8,128)(2,1)}, u32[]{:S(2)}, u32[]{:S(2)}) async-start(bf16[128,16,2048]{2,1,0:T(8,128)(2,1)} %bitcast.93), calls=%async_computation.3 | async-start | bytes 16777216 | tf_op jit(solution)/shard_map/all_to_all | solution.py:140
  332.2 0.3 reduce-scatter.2.cloned.1.call-start
  332.5 5.4 %fusion.54 = f32[1024,352]{0,1:T(8,128)} fusion(bf16[1024,2048]{1,0:T(8,128)(2,1)} %all-gather.5.cloned.1.call-done, bf16[2048,352]{0,1:T(8,128)(2,1)} %param.24), kind=kOutput, calls=%fused_computation.100 | convolution fusion | flops 1476395008 | bytes 7077888 | tf_op jit(solution)/shard_map/dot_general | solution.py:112
  337.9 9.4 %convolution_convert_fusion.1 = bf16[1024,2048]{1,0:T(8,128)(2,1)} fusion(bf16[352,2048]{1,0:T(8,128)(2,1)} %param.26, bf16[1024,2048]{1,0:T(8,128)(2,1)} %all-gather.5.cloned.1.call-done, bf16[2048,352]{0,1:T(8,128)(2,1)} %param.25, f32[1024,352]{0,1:T(8,128)} %fusion.54), kind=kOutput, calls=%fused_computation.34 | convolution fusion | flops 2957049856 | bytes 12713984 | tf_op jit(solution)/shard_map/dot_general | solution.py:116
  347.3 0.7 copy-done.4
  348.0 0.1 copy.36
  348.1 87.8 %all-to-all-done.2 = bf16[128,16,2048]{2,1,0:T(8,128)(2,1)} async-done(((bf16[128,16,2048]{2,1,0:T(8,128)(2,1)}), bf16[128,16,2048]{2,1,0:T(8,128)(2,1)}, u32[]{:S(2)}, u32[]{:S(2)}) %all-to-all-start.2) | async-done | bytes 8388640 | tf_op jit(solution)/shard_map/all_to_all | solution.py:140
  435.8 15.4 %gather_fusion.2 = bf16[768,2048]{1,0:T(8,128)(2,1)} fusion(bf16[64,2,16,2048]{3,2,1,0:T(8,128)(2,1)} %bitcast.16, s32[768]{0:T(1024)S(1)} %get-tuple-element.92), kind=kCustom, calls=%fused_computation.2 | custom fusion | bytes 6300672 | tf_op jit(solution)/shard_map/gather | solution.py:154
  451.3 15.5 %gather_fusion.1 = bf16[768,2048]{1,0:T(8,128)(2,1)} fusion(bf16[64,2,16,2048]{3,2,1,0:T(8,128)(2,1)} %bitcast.16, s32[768]{0:T(1024)S(1)} %get-tuple-element.91), kind=kCustom, calls=%fused_computation.1 | custom fusion | bytes 6300672 | tf_op jit(solution)/shard_map/gather | solution.py:153
  466.8 6.9 %convert_add_fusion = f32[768,2048]{1,0:T(8,128)} fusion(bf16[768,2048]{1,0:T(8,128)(2,1)} %gather_fusion.2, bf16[768,2048]{1,0:T(8,128)(2,1)} %gather_fusion.1), kind=kLoop, calls=%fused_computation.32 | loop fusion | flops 4718592 | bytes 12582912 | tf_op jit(solution)/shard_map/add | solution.py:155
  473.7 7.8 %add.123 = f32[128,6,2048]{2,1,0:T(8,128)} reshape(f32[768,2048]{1,0:T(8,128)} %convert_add_fusion) | data formatting | bytes 12582912 | tf_op jit(solution)/shard_map/add | solution.py:155
  481.5 7.6 %multiply_reduce_fusion = f32[128,2048]{1,0:T(8,128)} fusion(f32[128,6,2048]{2,1,0:T(8,128)} %add.123, f32[128,6]{1,0:T(8,128)S(1)} %copy.36), kind=kLoop, calls=%fused_computation.30 | loop fusion | flops 2883584 | bytes 7343104 | tf_op jit(solution)/shard_map/reduce_sum | solution.py:157
  489.1 2.3 add_convert_fusion
  (34 shorter events, 0.5 us)
Async XLA Ops:
  7.2 299.8 %copy-start = (bf16[1,704,2048]{2,1,0:T(8,128)(2,1)S(1)}, bf16[1,704,2048]{2,1,0:T(8,128)(2,1)}, u32[]{:S(2)}) copy-start(bf16[1,704,2048]{2,1,0:T(8,128)(2,1)} %param.29) | copy-start | bytes 8650756
  7.2 76.1 %all-gather.3.cloned.1.call-start = ((), (), s32[]{:S(2)}) async-start(), calls=%async_computation.4 | async-start | bytes 8912896 | tf_op jit(solution)/shard_map/all_gather | solution.py:97
  14.2 77.3 %copy-start.2 = (s32[64,6,128]{2,0,1:T(8,128)}, s32[64,6,128]{2,0,1:T(8,128)S(1)}, u32[]{:S(2)}) copy-start(s32[64,6,128]{2,0,1:T(8,128)S(1)} %reduce-window.19) | copy-start | bytes 589828
  92.8 69.3 %copy-start.1 = (bf16[128,2048]{1,0:T(8,128)(2,1)S(1)}, bf16[128,2048]{1,0:T(8,128)(2,1)}, u32[]{:S(2)}) copy-start(bf16[128,2048]{1,0:T(8,128)(2,1)} %param.16) | copy-start | bytes 1572868
  99.6 2.9 copy-start.3
  113.0 2.9 copy-start.3
  126.4 2.9 copy-start.3
  139.8 2.9 copy-start.3
  146.4 13.6 %all-to-all-start = ((bf16[16,128,128]{2,1,0:T(8,128)(2,1)}), bf16[16,128,128]{2,1,0:T(8,128)(2,1)}, u32[]{:S(2)}, u32[]{:S(2)}) async-start(bf16[16,128,128]{2,1,0:T(8,128)(2,1)} %bitcast.95), calls=%async_computation | async-start | bytes 1048576 | tf_op jit(solution)/shard_map/all_to_all | solution.py:106
  181.9 113.9 %all-to-all-start.1 = ((bf16[128,16,2048]{2,1,0:T(8,128)(2,1)}), bf16[128,16,2048]{2,1,0:T(8,128)(2,1)}, u32[]{:S(2)}, u32[]{:S(2)}) async-start(bf16[128,16,2048]{2,1,0:T(8,128)(2,1)} %bitcast.91), calls=%async_computation.2 | async-start | bytes 16777216 | tf_op jit(solution)/shard_map/all_to_all | solution.py:142
  192.3 140.2 %all-gather.5.cloned.1.call-start = ((), (), s32[]{:S(2)}) async-start(), calls=%async_computation.5 | async-start | bytes 4718592 | tf_op jit(solution)/shard_map/all_gather | solution.py:111
  326.0 109.8 %all-to-all-start.2 = ((bf16[128,16,2048]{2,1,0:T(8,128)(2,1)}), bf16[128,16,2048]{2,1,0:T(8,128)(2,1)}, u32[]{:S(2)}, u32[]{:S(2)}) async-start(bf16[128,16,2048]{2,1,0:T(8,128)(2,1)} %bitcast.93), calls=%async_computation.3 | async-start | bytes 16777216 | tf_op jit(solution)/shard_map/all_to_all | solution.py:140
  332.2 156.9 %reduce-scatter.2.cloned.1.call-start = ((), (), s32[]{:S(2)}) async-start(), calls=%async_computation.6 | async-start | bytes 4718592 | tf_op jit(solution)/shard_map/reduce_scatter | solution.py:115
  347.3 0.7 copy-start.4
Sparse Core Ops, SparseCore 0:
  10.8 72.4 all-gather.2
  195.4 107.2 all-gather.4
  347.4 100.0 reduce-scatter.1
where the time goes:
time: 507 us; the launch traced here: 498 us
  waiting for transfers between devices  263 us (52%)
  matrix products  86.1 us (17%)
  local copies, waits for them, and re-layouts  64.9 us (13%)
  other arithmetic  39.1 us (8%)
  starting transfers between devices  22.4 us (4%)
  between operations  14.3 us (3%)
  loops' own time  8.41 us (2%)
    all_to_all x1, waiting for transfers between devices, local(): lax.all_to_all(outbound, ('grp', 'ep'), split_axis=0, concat_axis=0, tile...  103 us
    all_to_all x1, waiting for transfers between devices, local(): lax.all_to_all(expert_rows(lax.all_to_all(outbound, ('grp', 'ep'), split_...  87.8 us
    all_gather x1, waiting for transfers between devices, local(): lax.all_gather(normed, 'ep', axis=0, tiled=True)  68.6 us
    dot_general x1, matrix products, expert_rows(): jnp.dot(hidden, down_half, preferred_element_type=jnp.float32)  19.1 us
    gather x1, local copies, waits for them, and re-layouts, local(): first_half = by_expert[flat_experts, 0, rank_in]  15.5 us
    gather x1, local copies, waits for them, and re-layouts, local(): second_half = by_expert[flat_experts, 1, rank_in]  15.4 us
    dot_general x4, matrix products, one_block(): jnp.einsum('hqk,khd->qhd', attn_probs, value_rows, preferred_element_type...  14.8 us
    dot_general x4, matrix products, one_block(): jnp.einsum('qhd,khd->hqk', query_block, key_rows, preferred_element_type=...  13.2 us
  transfers between devices with their start and end apart: 6, of which 4 were waited for; matrix products, arithmetic and copies ran while one was open for 21% of the time, Pallas kernels for 0%

commit v1 on v0

--- a/solution.py
+++ b/solution.py
@@ -94,7 +94,9 @@
     normed = rms_rows(hidden_in.astype(jnp.float32)).astype(jnp.bfloat16)
     w_joined = jnp.concatenate((w_query, w_key, w_value), axis=1)
     joined = jnp.dot(
-        lax.all_gather(normed, "ep", axis=0, tiled=True),
+        jnp.concatenate(
+            lax.all_to_all(jnp.stack([normed] * lax.axis_size("ep")), "ep", 0, 0), axis=0
+        ),
         w_joined,
         preferred_element_type=jnp.float32,
     ).astype(jnp.bfloat16)

time: 507 us -> 597 us (1.18)
  waiting for transfers between devices: 263 us -> 320 us
  starting transfers between devices: 22.4 us -> 52 us
    all_to_all x0 -> x1, waiting for transfers between devices: none -> 127 us  [local(): lax.all_to_all(jnp.stack([normed] * lax.axis_size('ep')), 'ep', 0, 0)]
    all_gather x1 -> x0, waiting for transfers between devices: 68.6 us -> none  [local(): lax.all_gather(normed, 'ep', axis=0, tiled=True)]
    all_to_all x1, starting transfers between devices: 5.48 us -> 25.5 us  [local(): lax.all_to_all(heads_local, 'ep', split_axis=0, concat_axis=1, tiled=True)]
    all_to_all x0 -> x1, starting transfers between devices: none -> 7.02 us  [local(): lax.all_to_all(jnp.stack([normed] * lax.axis_size('ep')), 'ep', 0, 0)]
  transfers between devices with their start and end apart: 6 -> 6, of which waited for: 4 -> 4; matrix products, arithmetic and copies ran while one was open for 21% -> 18% of each run, Pallas kernels for 0% -> 0%
where the time goes in v1:
time: 597 us; the launch traced here: 587 us
  waiting for transfers between devices  320 us (54%)
  matrix products  86.1 us (14%)
  local copies, waits for them, and re-layouts  67.8 us (11%)
  starting transfers between devices  52 us (9%)
  other arithmetic  38.3 us (6%)
  between operations  14.6 us (2%)
  loops' own time  8.41 us (1%)
    all_to_all x1, waiting for transfers between devices, local(): lax.all_to_all(jnp.stack([normed] * lax.axis_size('ep')), 'ep', 0, 0)  127 us
    all_to_all x1, waiting for transfers between devices, local(): lax.all_to_all(outbound, ('grp', 'ep'), split_axis=0, concat_axis=0, tile...  103 us
    all_to_all x1, waiting for transfers between devices, local(): lax.all_to_all(expert_rows(lax.all_to_all(outbound, ('grp', 'ep'), split_...  87.8 us
    all_to_all x1, starting transfers between devices, local(): lax.all_to_all(heads_local, 'ep', split_axis=0, concat_axis=1, tiled=True)  25.5 us
    dot_general x1, matrix products, expert_rows(): jnp.dot(hidden, down_half, preferred_element_type=jnp.float32)  19.1 us
    gather x1, local copies, waits for them, and re-layouts, local(): first_half = by_expert[flat_experts, 0, rank_in]  15.5 us
    gather x1, local copies, waits for them, and re-layouts, local(): second_half = by_expert[flat_experts, 1, rank_in]  15.4 us
    dot_general x4, matrix products, one_block(): jnp.einsum('hqk,khd->qhd', attn_probs, value_rows, preferred_element_type...  14.8 us
  transfers between devices with their start and end apart: 6, of which 4 were waited for; matrix products, arithmetic and copies ran while one was open for 18% of the time, Pallas kernels for 0%

profile of v1, /device:TPU:37, one launch (start us, length us, event | category | flops | bytes accessed | tf_op | source)
XLA Modules:
  0.0 587.3 jit_solution(4703839225427605317)
XLA Ops:
  7.2 1.4 fusion.33
  8.6 1.2 fusion.34
  9.8 4.3 stack.2
  14.1 7.0 %all-to-all-start = ((bf16[16,128,2048]{2,1,0:T(8,128)(2,1)}), bf16[16,128,2048]{2,1,0:T(8,128)(2,1)}, u32[]{:S(2)}, u32[]{:S(2)}) async-start(bf16[16,128,2048]{2,1,0:T(8,128)(2,1)} %stack.2), calls=%async_computation | async-start | bytes 16777216 | tf_op jit(solution)/shard_map/all_to_all | solution.py:98
  21.1 0.2 reduce-window.18
  21.3 0.1 copy.32
  21.4 0.1 eq.51
  21.6 1.8 reduce-window.19
  23.4 0.1 convert_reduce_fusion
  23.5 0.3 slice_reduce_fusion
  23.8 126.8 %all-to-all-done = bf16[16,128,2048]{2,1,0:T(8,128)(2,1)} async-done(((bf16[16,128,2048]{2,1,0:T(8,128)(2,1)}), bf16[16,128,2048]{2,1,0:T(8,128)(2,1)}, u32[]{:S(2)}, u32[]{:S(2)}) %all-to-all-start) | async-done | bytes 8388640 | tf_op jit(solution)/shard_map/all_to_all | solution.py:98
  150.6 8.3 %convolution_convert_fusion.2 = bf16[2048,384]{1,0:T(8,128)(2,1)S(1)} fusion(bf16[2048,2048]{1,0:T(8,128)(2,1)} %bitcast.2, bf16[2048,128]{1,0:T(8,128)(2,1)} %param.22, bf16[2048,128]{1,0:T(8,128)(2,1)} %param.21, bf16[2048,128]{1,0:T(8,128)(2,1)} %param.20), kind=kOutput, calls=%fused_computation.40 | convolution fusion | flops 3226730496 | bytes 11534336 | tf_op jit(solution)/shard_map/dot_general | solution.py:96
  158.9 1.3 slice_bitcast_fusion
  160.1 53.6 %while.12 = (s32[]{:T(128)}, bf16[4,512,1,128]{3,1,2,0:T(8,128)(2,1)}, s32[4]{0:T(128)S(1)}, s32[2048]{0:T(1024)S(1)}, bf16[2048,1,128]{2,0,1:T(8,128)(2,1)}, /*...) while((s32[]{:T(128)}, ...), condition=%wide.region_6.7_spmd.clone.clone, body=%wide.region_3.6_spmd.clone.clone.sunk | while | flops 570490880 | bytes 16046279 | solution.py:52
  160.1 0.7 dynamic_slice.28
  162.9 0.7 iota_add_fusion.2
  163.6 3.3 fusion.70
  166.9 2.9 fusion.71
  169.8 3.7 fusion.72
  173.5 0.7 dynamic_slice.28
  176.3 0.7 iota_add_fusion.2
  177.0 3.3 fusion.70
  180.4 2.9 fusion.71
  183.2 3.7 fusion.72
  186.9 0.7 dynamic_slice.28
  189.8 0.7 iota_add_fusion.2
  190.5 3.3 fusion.70
  193.8 2.9 fusion.71
  196.6 3.7 fusion.72
  200.3 0.7 dynamic_slice.28
  203.2 0.7 iota_add_fusion.2
  203.9 3.3 fusion.70
  207.2 2.9 fusion.71
  210.0 3.7 fusion.72
  213.7 25.5 %all-to-all-start.1 = ((bf16[16,128,128]{2,1,0:T(8,128)(2,1)}), bf16[16,128,128]{2,1,0:T(8,128)(2,1)}, u32[]{:S(2)}, u32[]{:S(2)}) async-start(bf16[16,128,128]{2,1,0:T(8,128)(2,1)} %bitcast.96), calls=%async_computation.1 | async-start | bytes 1048576 | tf_op jit(solution)/shard_map/all_to_all | solution.py:108
  239.3 0.1 eq.47
  239.4 0.1 reshape.224
  239.6 1.1 fusion.38
  240.7 3.4 scatter_custom_fusion
  244.1 2.0 all-to-all-done.1
  246.1 2.0 copy.31
  248.1 4.9 multiply_reduce_fusion.1
  253.0 1.1 multiply_convert_fusion.1
  254.2 1.1 concatenate.13
  255.2 6.0 %gather_fusion = bf16[1024,2048]{1,0:T(8,128)(2,1)} fusion(bf16[129,2048]{1,0:T(8,128)(2,1)S(1)} %concatenate.13, s32[1024]{0:T(1024)S(1)} %fusion.42), kind=kCustom, calls=%fused_computation | custom fusion | bytes 8392704 | tf_op jit(solution)/shard_map/gather | solution.py:135
  261.3 6.7 %broadcast_in_dim.43 = bf16[64,2,16,2048]{3,2,1,0:T(8,128)(2,1)} broadcast(bf16[64,16,2048]{2,1,0:T(8,128)(2,1)} %bitcast.93), dimensions={0,2,3} | broadcast | bytes 12582912 | tf_op jit(solution)/shard_map/broadcast_in_dim | solution.py:136
  268.0 13.0 %all-to-all-start.2 = ((bf16[128,16,2048]{2,1,0:T(8,128)(2,1)}), bf16[128,16,2048]{2,1,0:T(8,128)(2,1)}, u32[]{:S(2)}, u32[]{:S(2)}) async-start(bf16[128,16,2048]{2,1,0:T(8,128)(2,1)} %bitcast.92), calls=%async_computation.3 | async-start | bytes 16777216 | tf_op jit(solution)/shard_map/all_to_all | solution.py:144
  281.1 0.7 all-gather.2.cloned.1.call-update
  281.8 102.8 %all-to-all-done.2 = bf16[128,16,2048]{2,1,0:T(8,128)(2,1)} async-done(((bf16[128,16,2048]{2,1,0:T(8,128)(2,1)}), bf16[128,16,2048]{2,1,0:T(8,128)(2,1)}, u32[]{:S(2)}, u32[]{:S(2)}) %all-to-all-start.2) | async-done | bytes 8388640 | tf_op jit(solution)/shard_map/all_to_all | solution.py:144
  384.6 11.1 %fusion.24 = f32[2048,704]{0,1:T(8,128)} fusion(bf16[2048,2048]{1,0:T(8,128)(2,1)} %bitcast.12, bf16[1,2048,704]{1,2,0:T(8,128)(2,1)} %param.27), kind=kOutput, calls=%fused_computation.37 | convolution fusion | flops 5905580032 | bytes 17039360 | tf_op jit(solution)/shard_map/dot_general | solution.py:59
  395.7 19.1 %convolution_convert_fusion = bf16[2048,2048]{1,0:T(8,128)(2,1)} fusion(f32[2048,704]{0,1:T(8,128)} %fusion.24, bf16[2048,2048]{1,0:T(8,128)(2,1)} %bitcast.12, bf16[1,704,2048]{2,1,0:T(8,128)(2,1)S(1)} %copy-done, bf16[1,2048,704]{1,2,0:T(8,128)(2,1)} %param.28), kind=kOutput, calls=%fused_computation.31 | convolution fusion | flops 11824005120 | bytes 28311552 | tf_op jit(solution)/shard_map/dot_general | solution.py:62
  414.7 6.2 %all-to-all-start.3 = ((bf16[128,16,2048]{2,1,0:T(8,128)(2,1)}), bf16[128,16,2048]{2,1,0:T(8,128)(2,1)}, u32[]{:S(2)}, u32[]{:S(2)}) async-start(bf16[128,16,2048]{2,1,0:T(8,128)(2,1)} %bitcast.94), calls=%async_computation.4 | async-start | bytes 16777216 | tf_op jit(solution)/shard_map/all_to_all | solution.py:142
  420.9 0.3 reduce-scatter.2.cloned.1.call-start
  421.2 5.4 fusion.54
  426.6 9.4 %convolution_convert_fusion.1 = bf16[1024,2048]{1,0:T(8,128)(2,1)} fusion(bf16[352,2048]{1,0:T(8,128)(2,1)} %param.26, bf16[1024,2048]{1,0:T(8,128)(2,1)} %all-gather.2.cloned.1.call-done, bf16[2048,352]{0,1:T(8,128)(2,1)} %param.25, f32[1024,352]{0,1:T(8,128)} %fusion.54), kind=kOutput, calls=%fused_computation.34 | convolution fusion | flops 2957049856 | bytes 12713984 | tf_op jit(solution)/shard_map/dot_general | solution.py:118
  436.0 0.7 copy-done.5
  436.7 0.1 copy.36
  436.8 87.8 %all-to-all-done.3 = bf16[128,16,2048]{2,1,0:T(8,128)(2,1)} async-done(((bf16[128,16,2048]{2,1,0:T(8,128)(2,1)}), bf16[128,16,2048]{2,1,0:T(8,128)(2,1)}, u32[]{:S(2)}, u32[]{:S(2)}) %all-to-all-start.3) | async-done | bytes 8388640 | tf_op jit(solution)/shard_map/all_to_all | solution.py:142
  524.5 15.4 %gather_fusion.2 = bf16[768,2048]{1,0:T(8,128)(2,1)} fusion(bf16[64,2,16,2048]{3,2,1,0:T(8,128)(2,1)} %bitcast.17, s32[768]{0:T(1024)S(1)} %get-tuple-element.92), kind=kCustom, calls=%fused_computation.2 | custom fusion | bytes 6300672 | tf_op jit(solution)/shard_map/gather | solution.py:156
  540.0 15.5 %gather_fusion.1 = bf16[768,2048]{1,0:T(8,128)(2,1)} fusion(bf16[64,2,16,2048]{3,2,1,0:T(8,128)(2,1)} %bitcast.17, s32[768]{0:T(1024)S(1)} %get-tuple-element.91), kind=kCustom, calls=%fused_computation.1 | custom fusion | bytes 6300672 | tf_op jit(solution)/shard_map/gather | solution.py:155
  555.5 6.9 %convert_add_fusion = f32[768,2048]{1,0:T(8,128)} fusion(bf16[768,2048]{1,0:T(8,128)(2,1)} %gather_fusion.2, bf16[768,2048]{1,0:T(8,128)(2,1)} %gather_fusion.1), kind=kLoop, calls=%fused_computation.32 | loop fusion | flops 4718592 | bytes 12582912 | tf_op jit(solution)/shard_map/add | solution.py:157
  562.4 7.8 %add.123 = f32[128,6,2048]{2,1,0:T(8,128)} reshape(f32[768,2048]{1,0:T(8,128)} %convert_add_fusion) | data formatting | bytes 12582912 | tf_op jit(solution)/shard_map/add | solution.py:157
  570.2 7.6 %multiply_reduce_fusion = f32[128,2048]{1,0:T(8,128)} fusion(f32[128,6,2048]{2,1,0:T(8,128)} %add.123, f32[128,6]{1,0:T(8,128)S(1)} %copy.36), kind=kLoop, calls=%fused_computation.30 | loop fusion | flops 2883584 | bytes 7343104 | tf_op jit(solution)/shard_map/reduce_sum | solution.py:159
  577.8 2.3 add_convert_fusion
  (38 shorter events, 0.6 us)
Async XLA Ops:
  7.2 388.5 %copy-start = (bf16[1,704,2048]{2,1,0:T(8,128)(2,1)S(1)}, bf16[1,704,2048]{2,1,0:T(8,128)(2,1)}, u32[]{:S(2)}) copy-start(bf16[1,704,2048]{2,1,0:T(8,128)(2,1)} %param.29) | copy-start | bytes 8650756
  14.1 7.0 %copy-start.6 = (s32[1,5]{1,0:T(1,128)S(1)}, s32[1,5]{1,0:T(1,128)}, u32[]{:S(2)}) copy-start(s32[1,5]{1,0:T(1,128)} %param.17) | copy-start | bytes 64
  14.1 7.2 %copy-start.4 = (s32[128,6]{0,1:T(8,128)S(1)}, s32[128,6]{0,1:T(8,128)}, u32[]{:S(2)}) copy-start(s32[128,6]{0,1:T(8,128)} %param.18) | copy-start | bytes 9220
  14.1 136.5 %all-to-all-start = ((bf16[16,128,2048]{2,1,0:T(8,128)(2,1)}), bf16[16,128,2048]{2,1,0:T(8,128)(2,1)}, u32[]{:S(2)}, u32[]{:S(2)}) async-start(bf16[16,128,2048]{2,1,0:T(8,128)(2,1)} %stack.2), calls=%async_computation | async-start | bytes 16777216 | tf_op jit(solution)/shard_map/all_to_all | solution.py:98
  23.4 135.5 %copy-start.2 = (s32[64,6,128]{2,0,1:T(8,128)}, s32[64,6,128]{2,0,1:T(8,128)S(1)}, u32[]{:S(2)}) copy-start(s32[64,6,128]{2,0,1:T(8,128)S(1)} %reduce-window.19) | copy-start | bytes 589828
  160.1 88.0 %copy-start.1 = (bf16[128,2048]{1,0:T(8,128)(2,1)S(1)}, bf16[128,2048]{1,0:T(8,128)(2,1)}, u32[]{:S(2)}) copy-start(bf16[128,2048]{1,0:T(8,128)(2,1)} %param.16) | copy-start | bytes 1572868
  166.9 2.9 copy-start.3
  180.3 2.9 copy-start.3
  193.8 2.9 copy-start.3
  207.2 2.9 copy-start.3
  213.7 32.3 %all-to-all-start.1 = ((bf16[16,128,128]{2,1,0:T(8,128)(2,1)}), bf16[16,128,128]{2,1,0:T(8,128)(2,1)}, u32[]{:S(2)}, u32[]{:S(2)}) async-start(bf16[16,128,128]{2,1,0:T(8,128)(2,1)} %bitcast.96), calls=%async_computation.1 | async-start | bytes 1048576 | tf_op jit(solution)/shard_map/all_to_all | solution.py:108
  268.0 116.6 %all-to-all-start.2 = ((bf16[128,16,2048]{2,1,0:T(8,128)(2,1)}), bf16[128,16,2048]{2,1,0:T(8,128)(2,1)}, u32[]{:S(2)}, u32[]{:S(2)}) async-start(bf16[128,16,2048]{2,1,0:T(8,128)(2,1)} %bitcast.92), calls=%async_computation.3 | async-start | bytes 16777216 | tf_op jit(solution)/shard_map/all_to_all | solution.py:144
  281.0 140.2 %all-gather.2.cloned.1.call-start = ((), (), s32[]{:S(2)}) async-start(), calls=%async_computation.5 | async-start | bytes 4718592 | tf_op jit(solution)/shard_map/all_gather | solution.py:113
  414.7 109.8 %all-to-all-start.3 = ((bf16[128,16,2048]{2,1,0:T(8,128)(2,1)}), bf16[128,16,2048]{2,1,0:T(8,128)(2,1)}, u32[]{:S(2)}, u32[]{:S(2)}) async-start(bf16[128,16,2048]{2,1,0:T(8,128)(2,1)} %bitcast.94), calls=%async_computation.4 | async-start | bytes 16777216 | tf_op jit(solution)/shard_map/all_to_all | solution.py:142
  420.9 156.9 %reduce-scatter.2.cloned.1.call-start = ((), (), s32[]{:S(2)}) async-start(), calls=%async_computation.6 | async-start | bytes 4718592 | tf_op jit(solution)/shard_map/reduce_scatter | solution.py:117
  436.0 0.7 copy-start.5
Sparse Core Ops, SparseCore 0:
  284.1 107.2 all-gather.1
  436.1 100.0 reduce-scatter.1
